TPU v7x, 32 devices: a whole 2x2x4 slice. The times are simulated.
32 devices in a mesh: row: 8 (over y, x, core), col: 4 (over z).
Axes of the slice: x: 2, y: 2, z: 4, core: 2. Of those that a mesh axis runs over, the one named last changes fastest.
Arguments:
- amplitudes: bfloat16 [100, 100, 768], P(None, None, 'col'), may hold values from -6 to 6
- integrals: bfloat16 [768, 65536], P('col', 'row'), may hold values from -0.15625 to 0.15625
- blocks: int32 [8, 2], replicated, may hold values from 0 to 49, as said below
Outputs:
- residual: bfloat16 [32, 65536], P('col', 'row')
Inputs may be any that keep to these rules, and one draw needn't show every extreme that they name: `blocks`: each row is a block pair (I, J) with I <= J, all rows distinct; the pair (0, 49) is always among them.
All inputs are finite; a program needn't handle non-finite values.
Results may differ from a plain program's by a relative error of at most 0.001.
Values may be sent and summed in bfloat16 or wider, within the bound.
A program may use at most 128 MiB of HBM per device.

v0:
```python
import jax
import jax.numpy as jnp
from jax import lax
from jax.sharding import PartitionSpec as P

OB = 2
A_DEV = 32


def pick_rows(amplitudes, blocks):
    panel_width = amplitudes.shape[2]

    def one_block(pair_index):
        first_row = pair_index[0] * OB
        second_row = pair_index[1] * OB
        anchor = jnp.zeros((), jnp.int32)
        direct_rows = lax.dynamic_slice(
            amplitudes, (first_row, second_row, anchor), (OB, OB, panel_width)
        )
        swapped_rows = lax.dynamic_slice(
            amplitudes, (second_row, first_row, anchor), (OB, OB, panel_width)
        )
        return (
            direct_rows.reshape(OB * OB, panel_width),
            jnp.swapaxes(swapped_rows, 0, 1).reshape(OB * OB, panel_width),
        )

    direct_rows, swapped_rows = jax.vmap(one_block)(blocks)
    return (direct_rows.reshape(-1, panel_width), swapped_rows.reshape(-1, panel_width))


def on_device(amplitudes, integrals, blocks):
    forward, mirrored = pick_rows(amplitudes, blocks)
    depth = integrals.shape[0]
    full_width = integrals.shape[1] // A_DEV
    shaped = integrals.reshape(depth, A_DEV, full_width)
    received = lax.all_to_all(shaped, "row", split_axis=2, concat_axis=1, tiled=True)
    flipped = jnp.swapaxes(received, 1, 2).reshape(depth, A_DEV * full_width)
    summed = lax.psum_scatter(
        jnp.dot(forward, integrals, preferred_element_type=jnp.float32)
        + jnp.dot(mirrored, flipped, preferred_element_type=jnp.float32),
        "col",
        scatter_dimension=0,
        tiled=True,
    )
    return summed.astype(jnp.bfloat16)


def solution(mesh):
    return jax.shard_map(
        on_device,
        mesh=mesh,
        in_specs=(P(None, None, "col"), P("col", "row"), P()),
        out_specs=P("col", "row"),
        check_vma=False,
    )
```

profile of v0, /device:TPU:0, one launch (start us, length us, event | category | flops | bytes accessed | tf_op | source)
XLA Modules:
  0.0 135.0 jit_solution(56232211112688556)
XLA Ops:
  6.5 2.8 %copy.23 = bf16[24,8,32,256]{3,2,1,0:T(8,128)(2,1)S(1)} copy(bf16[24,8,32,256]{3,1,2,0:T(8,128)(2,1)} %bitcast.38) | data formatting | bytes 6291456
  9.4 6.3 %copy.16 = bf16[192,32,256]{0,1,2:T(8,128)(2,1)} copy(bf16[192,32,256]{2,1,0:T(8,128)(2,1)S(1)} %bitcast.37) | data formatting | bytes 6291456 | tf_op jit(solution)/shard_map/reshape | solution.py:36
  15.7 5.5 %all-to-all-start = ((bf16[192,32,256]{0,1,2:T(8,128)(2,1)}), bf16[192,32,256]{0,1,2:T(8,128)(2,1)}, u32[]{:S(2)}, u32[]{:S(2)}) async-start(bf16[192,32,256]{0,1,2:T(8,128)(2,1)} %copy.16), calls=%async_computation | async-start | bytes 8388608 | tf_op jit(solution)/shard_map/all_to_all | solution.py:37
  21.3 25.1 %while.2 = (s32[]{:T(128)}, bf16[100,100,192]{1,2,0:T(8,128)(2,1)}, s32[8,3]{0,1:T(4,128)S(1)}, bf16[8,2,2,192]{3,2,1,0:T(2,128)(2,1)S(1)}, s32[]{:T(128)}) while((s32[]{:T(128)}, bf16[100,100,192]{1,2,0:T(8,128)(2,1)}, s32[8,3]{0,1:T(4,128)S(1)}, bf16[8,2,2,192]{3,2,1,0:T(2,128)(2,1)S(1)}, s32[]{:T(128)}) %tuple.35), condition=%wide.while_cond, body=%wide.while_body.sunk | while | flops 2 | bytes 10365 | solution.py:17
  21.4 0.6 fusion.9
  21.9 2.3 %dynamic-slice_bitcast_fusion.2 = bf16[1,2,2,192]{2,3,1,0:T(8,128)(2,1)S(1)} fusion(bf16[100,100,192]{1,2,0:T(8,128)(2,1)} %get-tuple-element.114, s32[]{:T(128)} %bitcast.30, s32[]{:T(128)} %bitcast.31), kind=kLoop, calls=%fused_computation.clone.1 | loop fusion | bytes 3080 | tf_op jit(solution)/shard_map/vmap()/gather
  24.3 0.1 copy.26
  24.5 0.6 fusion.9
  25.1 2.3 %dynamic-slice_bitcast_fusion.2 = bf16[1,2,2,192]{2,3,1,0:T(8,128)(2,1)S(1)} fusion(bf16[100,100,192]{1,2,0:T(8,128)(2,1)} %get-tuple-element.114, s32[]{:T(128)} %bitcast.30, s32[]{:T(128)} %bitcast.31), kind=kLoop, calls=%fused_computation.clone.1 | loop fusion | bytes 3080 | tf_op jit(solution)/shard_map/vmap()/gather
  27.4 0.1 copy.26
  27.6 0.6 fusion.9
  28.2 2.3 %dynamic-slice_bitcast_fusion.2 = bf16[1,2,2,192]{2,3,1,0:T(8,128)(2,1)S(1)} fusion(bf16[100,100,192]{1,2,0:T(8,128)(2,1)} %get-tuple-element.114, s32[]{:T(128)} %bitcast.30, s32[]{:T(128)} %bitcast.31), kind=kLoop, calls=%fused_computation.clone.1 | loop fusion | bytes 3080 | tf_op jit(solution)/shard_map/vmap()/gather
  30.6 0.1 copy.26
  30.8 0.6 fusion.9
  31.4 2.3 %dynamic-slice_bitcast_fusion.2 = bf16[1,2,2,192]{2,3,1,0:T(8,128)(2,1)S(1)} fusion(bf16[100,100,192]{1,2,0:T(8,128)(2,1)} %get-tuple-element.114, s32[]{:T(128)} %bitcast.30, s32[]{:T(128)} %bitcast.31), kind=kLoop, calls=%fused_computation.clone.1 | loop fusion | bytes 3080 | tf_op jit(solution)/shard_map/vmap()/gather
  33.9 0.6 fusion.9
  34.5 2.3 %dynamic-slice_bitcast_fusion.2 = bf16[1,2,2,192]{2,3,1,0:T(8,128)(2,1)S(1)} fusion(bf16[100,100,192]{1,2,0:T(8,128)(2,1)} %get-tuple-element.114, s32[]{:T(128)} %bitcast.30, s32[]{:T(128)} %bitcast.31), kind=kLoop, calls=%fused_computation.clone.1 | loop fusion | bytes 3080 | tf_op jit(solution)/shard_map/vmap()/gather
  37.0 0.6 fusion.9
  37.6 2.3 %dynamic-slice_bitcast_fusion.2 = bf16[1,2,2,192]{2,3,1,0:T(8,128)(2,1)S(1)} fusion(bf16[100,100,192]{1,2,0:T(8,128)(2,1)} %get-tuple-element.114, s32[]{:T(128)} %bitcast.30, s32[]{:T(128)} %bitcast.31), kind=kLoop, calls=%fused_computation.clone.1 | loop fusion | bytes 3080 | tf_op jit(solution)/shard_map/vmap()/gather
  40.2 0.6 fusion.9
  40.8 2.3 %dynamic-slice_bitcast_fusion.2 = bf16[1,2,2,192]{2,3,1,0:T(8,128)(2,1)S(1)} fusion(bf16[100,100,192]{1,2,0:T(8,128)(2,1)} %get-tuple-element.114, s32[]{:T(128)} %bitcast.30, s32[]{:T(128)} %bitcast.31), kind=kLoop, calls=%fused_computation.clone.1 | loop fusion | bytes 3080 | tf_op jit(solution)/shard_map/vmap()/gather
  43.3 0.6 fusion.9
  43.9 2.3 %dynamic-slice_bitcast_fusion.2 = bf16[1,2,2,192]{2,3,1,0:T(8,128)(2,1)S(1)} fusion(bf16[100,100,192]{1,2,0:T(8,128)(2,1)} %get-tuple-element.114, s32[]{:T(128)} %bitcast.30, s32[]{:T(128)} %bitcast.31), kind=kLoop, calls=%fused_computation.clone.1 | loop fusion | bytes 3080 | tf_op jit(solution)/shard_map/vmap()/gather
  46.4 28.8 %while.3 = (s32[]{:T(128)}, bf16[100,100,192]{1,2,0:T(8,128)(2,1)}, s32[8,3]{0,1:T(4,128)S(1)}, bf16[8,2,2,192]{2,3,1,0:T(8,128)(2,1)}, s32[]{:T(128)}) while((s32[]{:T(128)}, bf16[100,100,192]{1,2,0:T(8,128)(2,1)}, s32[8,3]{0,1:T(4,128)S(1)}, bf16[8,2,2,192]{2,3,1,0:T(8,128)(2,1)}, s32[]{:T(128)}) %tuple.43), condition=%wide.while_cond.1, body=%wide.while_body.1.sunk | while | flops 2 | bytes 197749 | solution.py:20
  46.5 0.6 fusion.10
  47.1 2.9 %bitcast_dynamic-update-slice_fusion.2 = bf16[8,2,2,192]{2,3,1,0:T(8,128)(2,1)} fusion(bf16[8,2,2,192]{2,3,1,0:T(8,128)(2,1)} %get-tuple-element.126, s32[]{:T(128)S(6)} %copy.37, bf16[100,100,192]{1,2,0:T(8,128)(2,1)} %get-tuple-element.129, s32[]{:T(128)} %bitcast.33, s32[]{:T(128)} %bitcast.34), kind=kLoop, calls=%fused_computation.3.clone.1 | loop fusion | bytes 197636 | tf_op jit(solution)/shard_map/vmap()/gather
  50.1 0.6 fusion.10
  50.7 2.9 %bitcast_dynamic-update-slice_fusion.2 = bf16[8,2,2,192]{2,3,1,0:T(8,128)(2,1)} fusion(bf16[8,2,2,192]{2,3,1,0:T(8,128)(2,1)} %get-tuple-element.126, s32[]{:T(128)S(6)} %copy.37, bf16[100,100,192]{1,2,0:T(8,128)(2,1)} %get-tuple-element.129, s32[]{:T(128)} %bitcast.33, s32[]{:T(128)} %bitcast.34), kind=kLoop, calls=%fused_computation.3.clone.1 | loop fusion | bytes 197636 | tf_op jit(solution)/shard_map/vmap()/gather
  53.7 0.6 fusion.10
  54.3 2.9 %bitcast_dynamic-update-slice_fusion.2 = bf16[8,2,2,192]{2,3,1,0:T(8,128)(2,1)} fusion(bf16[8,2,2,192]{2,3,1,0:T(8,128)(2,1)} %get-tuple-element.126, s32[]{:T(128)S(6)} %copy.37, bf16[100,100,192]{1,2,0:T(8,128)(2,1)} %get-tuple-element.129, s32[]{:T(128)} %bitcast.33, s32[]{:T(128)} %bitcast.34), kind=kLoop, calls=%fused_computation.3.clone.1 | loop fusion | bytes 197636 | tf_op jit(solution)/shard_map/vmap()/gather
  57.3 0.6 fusion.10
  57.9 2.9 %bitcast_dynamic-update-slice_fusion.2 = bf16[8,2,2,192]{2,3,1,0:T(8,128)(2,1)} fusion(bf16[8,2,2,192]{2,3,1,0:T(8,128)(2,1)} %get-tuple-element.126, s32[]{:T(128)S(6)} %copy.37, bf16[100,100,192]{1,2,0:T(8,128)(2,1)} %get-tuple-element.129, s32[]{:T(128)} %bitcast.33, s32[]{:T(128)} %bitcast.34), kind=kLoop, calls=%fused_computation.3.clone.1 | loop fusion | bytes 197636 | tf_op jit(solution)/shard_map/vmap()/gather
  60.9 0.6 fusion.10
  61.5 2.9 %bitcast_dynamic-update-slice_fusion.2 = bf16[8,2,2,192]{2,3,1,0:T(8,128)(2,1)} fusion(bf16[8,2,2,192]{2,3,1,0:T(8,128)(2,1)} %get-tuple-element.126, s32[]{:T(128)S(6)} %copy.37, bf16[100,100,192]{1,2,0:T(8,128)(2,1)} %get-tuple-element.129, s32[]{:T(128)} %bitcast.33, s32[]{:T(128)} %bitcast.34), kind=kLoop, calls=%fused_computation.3.clone.1 | loop fusion | bytes 197636 | tf_op jit(solution)/shard_map/vmap()/gather
  64.5 0.6 fusion.10
  65.0 3.0 %bitcast_dynamic-update-slice_fusion.2 = bf16[8,2,2,192]{2,3,1,0:T(8,128)(2,1)} fusion(bf16[8,2,2,192]{2,3,1,0:T(8,128)(2,1)} %get-tuple-element.126, s32[]{:T(128)S(6)} %copy.37, bf16[100,100,192]{1,2,0:T(8,128)(2,1)} %get-tuple-element.129, s32[]{:T(128)} %bitcast.33, s32[]{:T(128)} %bitcast.34), kind=kLoop, calls=%fused_computation.3.clone.1 | loop fusion | bytes 197636 | tf_op jit(solution)/shard_map/vmap()/gather
  68.1 0.6 fusion.10
  68.6 2.9 %bitcast_dynamic-update-slice_fusion.2 = bf16[8,2,2,192]{2,3,1,0:T(8,128)(2,1)} fusion(bf16[8,2,2,192]{2,3,1,0:T(8,128)(2,1)} %get-tuple-element.126, s32[]{:T(128)S(6)} %copy.37, bf16[100,100,192]{1,2,0:T(8,128)(2,1)} %get-tuple-element.129, s32[]{:T(128)} %bitcast.33, s32[]{:T(128)} %bitcast.34), kind=kLoop, calls=%fused_computation.3.clone.1 | loop fusion | bytes 197636 | tf_op jit(solution)/shard_map/vmap()/gather
  71.7 0.6 fusion.10
  72.2 2.9 %bitcast_dynamic-update-slice_fusion.2 = bf16[8,2,2,192]{2,3,1,0:T(8,128)(2,1)} fusion(bf16[8,2,2,192]{2,3,1,0:T(8,128)(2,1)} %get-tuple-element.126, s32[]{:T(128)S(6)} %copy.37, bf16[100,100,192]{1,2,0:T(8,128)(2,1)} %get-tuple-element.129, s32[]{:T(128)} %bitcast.33, s32[]{:T(128)} %bitcast.34), kind=kLoop, calls=%fused_computation.3.clone.1 | loop fusion | bytes 197636 | tf_op jit(solution)/shard_map/vmap()/gather
  75.2 1.5 %copy.15 = bf16[8,2,2,192]{3,2,1,0:T(2,128)(2,1)S(1)} copy(bf16[8,2,2,192]{1,3,2,0:T(8,128)(2,1)} %bitcast.40) | data formatting | bytes 24576 | tf_op jit(solution)/shard_map/vmap()/transpose | solution.py:25
  76.8 1.8 %fusion.2 = f32[32,8192]{1,0:T(8,128)} fusion(bf16[32,192]{1,0:T(8,128)(2,1)S(1)} %reshape.12, bf16[192,8192]{1,0:T(8,128)(2,1)S(1)} %copy-done), kind=kOutput, calls=%fused_computation.12 | convolution fusion | flops 100663296 | bytes 4206592 | tf_op jit(solution)/shard_map/dot_general | solution.py:40
  78.5 6.7 %copy.18 = bf16[192,8,32,32]{0,3,2,1:T(8,128)(2,1)} copy(bf16[192,8,32,32]{0,2,3,1:T(8,128)(2,1)} %bitcast.3) | data formatting | bytes 6291456 | tf_op jit(solution)/shard_map/all_to_all | solution.py:37
  85.2 7.5 %copy.19 = bf16[192,32,256]{2,1,0:T(8,128)(2,1)S(1)} copy(bf16[192,32,256]{0,1,2:T(8,128)(2,1)} %bitcast.35) | data formatting | bytes 6291456 | tf_op jit(solution)/shard_map/transpose | solution.py:38
  92.8 2.2 %copy.24 = bf16[24,8,32,256]{3,1,2,0:T(8,128)(2,1)S(1)} copy(bf16[24,8,32,256]{3,2,1,0:T(8,128)(2,1)S(1)} %bitcast.36) | data formatting | bytes 6291456
  95.0 1.7 %convolution_add_fusion = f32[32,8192]{1,0:T(8,128)} fusion(f32[32,8192]{1,0:T(8,128)S(1)} %copy-done.1, bf16[32,192]{1,0:T(8,128)(2,1)S(1)} %reshape.13, bf16[192,8192]{1,0:T(8,128)(2,1)S(1)} %bitcast.39), kind=kOutput, calls=%fused_computation.5 | convolution fusion | flops 100925440 | bytes 5255168 | tf_op jit(solution)/shard_map/dot_general | solution.py:41
  96.7 29.9 %reduce-scatter.2.cloned.1.call-done = f32[8,8192]{1,0:T(8,128)} async-done(((f32[32,8192]{1,0:T(8,128)}), f32[8,8192]{1,0:T(8,128)}) %reduce-scatter.2.cloned.1.call-update) | async-done | bytes 262160 | tf_op jit(solution)/shard_map/reduce_scatter | solution.py:39
  126.6 1.6 %convert_element_type.3 = bf16[8,8192]{1,0:T(8,128)(2,1)} convert(f32[8,8192]{1,0:T(8,128)} %reduce-scatter.2.cloned.1.call-done) | non-fusion elementwise | flops 65536 | bytes 393216 | tf_op jit(solution)/shard_map/convert_element_type | solution.py:46
  (45 shorter events, 2.0 us)
Async XLA Ops:
  15.7 5.5 %copy-start.2 = (s32[8,2]{0,1:T(2,128)S(1)}, s32[8,2]{0,1:T(2,128)}, u32[]{:S(2)}) copy-start(s32[8,2]{0,1:T(2,128)} %param.5) | copy-start | bytes 196
  15.7 61.1 %copy-start = (bf16[192,8192]{1,0:T(8,128)(2,1)S(1)}, bf16[192,8192]{1,0:T(8,128)(2,1)}, u32[]{:S(2)}) copy-start(bf16[192,8192]{1,0:T(8,128)(2,1)} %param.4) | copy-start | bytes 9437188
  15.7 62.8 %all-to-all-start = ((bf16[192,32,256]{0,1,2:T(8,128)(2,1)}), bf16[192,32,256]{0,1,2:T(8,128)(2,1)}, u32[]{:S(2)}, u32[]{:S(2)}) async-start(bf16[192,32,256]{0,1,2:T(8,128)(2,1)} %copy.16), calls=%async_computation | async-start | bytes 8388608 | tf_op jit(solution)/shard_map/all_to_all | solution.py:37
  21.2 105.4 %reduce-scatter.2.cloned.1.call-start = ((), (), s32[]{:S(2)}) async-start(), calls=%async_computation.2 | async-start | bytes 1310720 | tf_op jit(solution)/shard_map/reduce_scatter | solution.py:39
  92.8 2.2 %copy-start.1 = (f32[32,8192]{1,0:T(8,128)S(1)}, f32[32,8192]{1,0:T(8,128)}, u32[]{:S(2)}) copy-start(f32[32,8192]{1,0:T(8,128)} %fusion.2) | copy-start | bytes 3145732
Sparse Core Ops, SparseCore 0:
  96.8 29.6 reduce-scatter.1
where the time goes:
time: 136 us; the launch traced here: 135 us
  local copies, waits for them, and re-layouts  80.9 us (59%)
  waiting for transfers between devices  29.9 us (22%)
  between operations  13.5 us (10%)
  starting transfers between devices  5.5 us (4%)
  matrix products  3.42 us (3%)
  other arithmetic  1.64 us (1%)
    gather x64, local copies, waits for them, and re-layouts  53.7 us
    reduce_scatter x1, waiting for transfers between devices, on_device(): lax.psum_scatter(jnp.dot(forward, integrals, preferred_element_type=jnp.f...  29.9 us
    transpose x1, local copies, waits for them, and re-layouts, on_device(): flipped = jnp.swapaxes(received, 1, 2).reshape(depth, A_DEV * full_width)  7.52 us
    all_to_all x1, local copies, waits for them, and re-layouts, on_device(): lax.all_to_all(shaped, 'row', split_axis=2, concat_axis=1, tiled=True)  6.71 us
    reshape x1, local copies, waits for them, and re-layouts, on_device(): shaped = integrals.reshape(depth, A_DEV, full_width)  6.32 us
    all_to_all x1, starting transfers between devices, on_device(): lax.all_to_all(shaped, 'row', split_axis=2, concat_axis=1, tiled=True)  5.46 us
    unnamed x8, local copies, waits for them, and re-layouts  5.06 us
  transfers between devices with their start and end apart: 2, of which 1 were waited for; matrix products, arithmetic and copies ran while one was open for 42% of the time, Pallas kernels for 0%

commit v1 on v0

v1 whole, which is shorter than its diff:
```python
import functools
import math

import jax
import jax.numpy as jnp
from jax import lax
from jax.experimental import pallas as pl
from jax.experimental.pallas import tpu as pltpu
from jax.sharding import PartitionSpec as P

OB = 2
LANES = 128
ROWS = 8


def ladder_kernel(
    n_row, n_col, a_dev,
    blocks, amp_hbm, int_hbm, out_ref,
    amp, ints, lhs, prod, turned, inbox, from_left, from_right,
    amp_sem, int_sem, x_send, x_recv, r_send, r_recv, l_send, l_recv,
):
    row = lax.axis_index("row")
    col = lax.axis_index("col")
    pairs = lhs.shape[0] // 2
    width = a_dev * n_row
    tiles = width // LANES
    per_tile = LANES // a_dev
    share = pairs // n_col
    groups = share // per_tile
    occ = amp.shape[2]
    n_parts = int_sem.shape[0]
    part = ints.shape[1] // n_parts

    barrier = pltpu.get_barrier_semaphore()

    def greet(p, carry):
        pl.semaphore_signal(barrier, inc=1, device_id={"row": lax.rem(row + p, n_row)})
        return carry

    lax.fori_loop(1, n_row, greet, 0)

    @pl.when(col > 0)
    def _():
        pl.semaphore_signal(barrier, inc=1, device_id={"col": col - 1})

    @pl.when(col < n_col - 1)
    def _():
        pl.semaphore_signal(barrier, inc=1, device_id={"col": col + 1})

    amp_copy = pltpu.make_async_copy(amp_hbm, amp, amp_sem)
    amp_copy.start()
    int_copies = []
    for i in range(n_parts):
        cut = pl.ds(i * part, part)
        copy = pltpu.make_async_copy(int_hbm.at[:, cut], ints.at[:, cut], int_sem.at[i])
        copy.start()
        int_copies.append(copy)

    amp_copy.wait()
    spot_row = lax.broadcasted_iota(jnp.int32, (ROWS, occ), 0)
    spot_col = lax.broadcasted_iota(jnp.int32, (ROWS, occ), 1)

    def take(spots, plane):
        hit = jnp.zeros((ROWS, occ), jnp.bool_)
        for at, column in spots:
            hit = hit | ((spot_row == at) & (spot_col == column))
        chosen = jnp.where(hit, 1.0, 0.0).astype(amp.dtype)
        return lax.dot_general(
            chosen, amp[plane], (((1,), (1,)), ((), ())), preferred_element_type=jnp.float32
        )

    per_rows = ROWS // (OB * OB)
    for tile in range(pairs // ROWS):
        direct = jnp.zeros((ROWS, lhs.shape[1]), jnp.float32)
        swapped = direct
        for k in range(per_rows):
            upper = blocks[0, tile * per_rows + k] * OB
            lower = blocks[1, tile * per_rows + k] * OB
            base = k * OB * OB
            for m in range(OB):
                direct += take([(base + m * OB + v, lower + v) for v in range(OB)], upper + m)
                swapped += take([(base + u * OB + m, upper + u) for u in range(OB)], lower + m)
        lhs[tile * ROWS:(tile + 1) * ROWS, :] = direct
        lhs[pairs + tile * ROWS:pairs + (tile + 1) * ROWS, :] = swapped
    rows = lhs[...].astype(jnp.bfloat16)

    for i in range(n_parts):
        int_copies[i].wait()

        def one(step, carry, i=i):
            a = i * (part // width) + step
            panel = ints[:, pl.ds(pl.multiple_of(a * width, width), width)]
            got = jnp.dot(rows, panel, preferred_element_type=jnp.float32)
            for t in range(tiles):
                prod[t, pl.ds(a, 2 * pairs, stride=a_dev), :] = got[:, t * LANES:(t + 1) * LANES]
            return carry

        lax.fori_loop(0, part // width, one, 0, unroll=2)

    n_near = jnp.where(col > 0, 1, 0) + jnp.where(col < n_col - 1, 1, 0)
    pl.semaphore_wait(barrier, n_row - 1 + n_near)

    def order(s):
        return jnp.where(col < n_col // 2, n_col - 1 - s, s)

    def x_copy(d, p):
        peer = lax.rem(row + p, n_row)
        return pltpu.make_async_remote_copy(
            src_ref=turned.at[pl.ds(d * groups, groups), pl.ds(pl.multiple_of(peer * a_dev, a_dev), a_dev), :],
            dst_ref=inbox.at[d, row],
            send_sem=x_send.at[d, p],
            recv_sem=x_recv.at[d, p],
            device_id={"row": peer},
        )

    chunk = share * a_dev

    def mine(d, t, start=0, size=chunk):
        return prod.at[t, pl.ds(pl.multiple_of(d * chunk + start, a_dev), size)]

    def right_copy(d, t):
        return pltpu.make_async_remote_copy(
            src_ref=mine(d, t), dst_ref=from_left.at[d, t],
            send_sem=r_send.at[d, t], recv_sem=r_recv.at[d, t],
            device_id={"col": col + 1},
        )

    def left_copy(d, t):
        return pltpu.make_async_remote_copy(
            src_ref=mine(d, t), dst_ref=from_right.at[d, t],
            send_sem=l_send.at[d, t], recv_sem=l_recv.at[d, t],
            device_id={"col": col - 1},
        )

    def turn(s, carry):
        d = order(s)
        for g in range(groups):
            start = (pairs + d * share + g * per_tile) * a_dev
            for t in range(tiles):
                block = prod[t, pl.ds(pl.multiple_of(start, LANES), LANES), :]
                turned[d * groups + g, t * LANES:(t + 1) * LANES, :] = block.T

        def post(p, inner):
            x_copy(d, p).start()
            return inner

        lax.fori_loop(1, n_row, post, 0)
        return carry

    lax.fori_loop(0, n_col, turn, 0)

    piece = lax.broadcasted_iota(jnp.int32, (a_dev, LANES), 1) // a_dev

    def combine(s, carry):
        d = order(s)
        for g in range(groups):
            inbox[d, row, g] = turned[d * groups + g, pl.ds(pl.multiple_of(row * a_dev, a_dev), a_dev), :]
        for t in range(tiles):
            for j in range(per_tile):
                source = t * per_tile + j

                @pl.when(source != row)
                def _(source=source):
                    x_copy(d, lax.rem(row - source + n_row, n_row)).wait_recv()

            for g in range(groups):
                parts = [inbox[d, t * per_tile + j, g] for j in range(per_tile)]
                for q in range(per_tile):
                    merged = parts[q] if q == 0 else pltpu.roll(parts[0], (-q * a_dev) % LANES, 1)
                    for j in range(1, per_tile):
                        shift = ((j - q) * a_dev) % LANES
                        moved = pltpu.roll(parts[j], shift, 1) if shift else parts[j]
                        merged = jnp.where(piece == j, moved, merged)
                    here = mine(d, t, (g * per_tile + q) * a_dev, a_dev)
                    here[...] = here[...] + merged

            @pl.when(d > col)
            def _():
                @pl.when(col > 0)
                def _():
                    right_copy(d, t).wait_recv()
                    mine(d, t)[...] = mine(d, t)[...] + from_left[d, t]

                right_copy(d, t).start()

            @pl.when(d < col)
            def _():
                @pl.when(col < n_col - 1)
                def _():
                    left_copy(d, t).wait_recv()
                    mine(d, t)[...] = mine(d, t)[...] + from_right[d, t]

                left_copy(d, t).start()

        return carry

    lax.fori_loop(0, n_col, combine, 0)

    for t in range(tiles):
        @pl.when(col > 0)
        def _(t=t):
            right_copy(col, t).wait_recv()
            mine(col, t)[...] = mine(col, t)[...] + from_left[col, t]

        @pl.when(col < n_col - 1)
        def _(t=t):
            left_copy(col, t).wait_recv()
            mine(col, t)[...] = mine(col, t)[...] + from_right[col, t]

        for a in range(a_dev):
            value = prod[t, pl.ds(col * chunk + a, share, stride=a_dev), :]
            at = a * width + t * LANES
            out_ref[:, at:at + LANES] = value.astype(out_ref.dtype)

    def finish(d, carry):
        def sent(p, inner):
            x_copy(d, p).wait_send()
            return inner

        lax.fori_loop(1, n_row, sent, 0)
        for t in range(tiles):
            @pl.when(d > col)
            def _(t=t):
                right_copy(d, t).wait_send()

            @pl.when(d < col)
            def _(t=t):
                left_copy(d, t).wait_send()

        return carry

    lax.fori_loop(0, n_col, finish, 0)


def on_device(n_row, n_col, amplitudes, integrals, blocks):
    amplitudes = jnp.swapaxes(amplitudes, 1, 2)
    blocks = blocks.T
    depth, local = integrals.shape
    width = math.isqrt(local * n_row)
    a_dev = width // n_row
    pairs = blocks.shape[1] * OB * OB
    tiles = width // LANES
    share = pairs // n_col
    groups = share * a_dev // LANES
    n_parts = 4
    f32 = jnp.float32
    dma = pltpu.SemaphoreType.DMA
    return pl.pallas_call(
        functools.partial(ladder_kernel, n_row, n_col, a_dev),
        out_shape=jax.ShapeDtypeStruct((share, local), jnp.bfloat16),
        in_specs=[
            pl.BlockSpec(memory_space=pltpu.SMEM),
            pl.BlockSpec(memory_space=pl.ANY),
            pl.BlockSpec(memory_space=pl.ANY),
        ],
        out_specs=pl.BlockSpec(memory_space=pltpu.VMEM),
        scratch_shapes=[
            pltpu.VMEM(amplitudes.shape, amplitudes.dtype),
            pltpu.VMEM(integrals.shape, integrals.dtype),
            pltpu.VMEM((2 * pairs, depth), f32),
            pltpu.VMEM((tiles, 2 * pairs * a_dev, LANES), f32),
            pltpu.VMEM((n_col * groups, width, LANES), f32),
            pltpu.VMEM((n_col, n_row, groups, a_dev, LANES), f32),
            pltpu.VMEM((n_col, tiles, share * a_dev, LANES), f32),
            pltpu.VMEM((n_col, tiles, share * a_dev, LANES), f32),
            dma(()),
            dma((n_parts,)),
            dma((n_col, n_row)),
            dma((n_col, n_row)),
            dma((n_col, tiles)),
            dma((n_col, tiles)),
            dma((n_col, tiles)),
            dma((n_col, tiles)),
        ],
        compiler_params=pltpu.CompilerParams(
            collective_id=0, has_side_effects=True, vmem_limit_bytes=67043328
        ),
    )(blocks, amplitudes, integrals)


def solution(mesh):
    return jax.shard_map(
        functools.partial(on_device, mesh.shape["row"], mesh.shape["col"]),
        mesh=mesh,
        in_specs=(P(None, None, "col"), P("col", "row"), P()),
        out_specs=P("col", "row"),
        check_vma=False,
    )
```

time: 136 us -> 41.4 us (0.30)
  local copies, waits for them, and re-layouts: 80.9 us -> 1.57 us
  Pallas kernels: 0 us -> 39.7 us
  waiting for transfers between devices: 29.9 us -> 0 us
  between operations: 13.5 us -> 0.01 us
  starting transfers between devices: 5.5 us -> 0 us
  matrix products: 3.42 us -> 0 us
  other arithmetic: 1.64 us -> 0 us
    gather x64 -> x0, local copies, waits for them, and re-layouts: 53.7 us -> none
    pallas_call x0 -> x1, Pallas kernels: none -> 39.7 us  [on_device(): pl.pallas_call(functools.partial(ladder_kernel, n_row, n_col, a_dev), out...]
    reduce_scatter x1 -> x0, waiting for transfers between devices: 29.9 us -> none  [on_device(): lax.psum_scatter(jnp.dot(forward, integrals, preferred_element_type=jnp.f...]
    transpose x2 -> x0, local copies, waits for them, and re-layouts: 9.04 us -> none  [the longest x1 7.52 us: on_device(): flipped = jnp.swapaxes(received, 1, 2).reshape(depth, A_DEV * full_width)]
    all_to_all x1 -> x0, local copies, waits for them, and re-layouts: 6.71 us -> none  [on_device(): lax.all_to_all(shaped, 'row', split_axis=2, concat_axis=1, tiled=True)]
    reshape x3 -> x0, local copies, waits for them, and re-layouts: 6.39 us -> none  [the longest x1 6.32 us: on_device(): shaped = integrals.reshape(depth, A_DEV, full_width)]
    all_to_all x1 -> x0, starting transfers between devices: 5.46 us -> none  [on_device(): lax.all_to_all(shaped, 'row', split_axis=2, concat_axis=1, tiled=True)]
    unnamed x8 -> x1, local copies, waits for them, and re-layouts: 5.06 us -> 1.57 us
  transfers between devices with their start and end apart: 2 -> 0, of which waited for: 1 -> 0; matrix products, arithmetic and copies ran while one was open for 42% -> 0% of each run, Pallas kernels for 0% -> 0%
where the time goes in v1:
time: 41.4 us; the launch traced here: 41.3 us
  Pallas kernels  39.7 us (96%)
  local copies, waits for them, and re-layouts  1.57 us (4%)
    pallas_call x1, Pallas kernels, on_device(): pl.pallas_call(functools.partial(ladder_kernel, n_row, n_col, a_dev), out...  39.7 us
    unnamed x1, local copies, waits for them, and re-layouts  1.57 us

profile of v1, /device:TPU:0, one launch (start us, length us, event | category | flops | bytes accessed | tf_op | source)
XLA Modules:
  0.0 41.3 jit_solution(9229161922792425425)
XLA Ops:
  0.0 39.7 %shard_map.37 = bf16[8,8192]{1,0:T(8,128)(2,1)} custom-call(s32[2,8]{1,0:T(2,128)} %bitcast.3, bf16[100,192,100]{2,1,0:T(8,128)(2,1)} %bitcast.2, bf16[192,8192]{1,0:T(8,128)(2,1)} %int_hbm.1), custom_call_target="tpu_custom_call" | custom-call | tf_op jit(solution)/shard_map/pallas_call | solution.py:248
  39.7 1.6 %copy.5 = bf16[8,8192]{1,0:T(8,128)(2,1)} copy(bf16[8,8192]{1,0:T(8,128)(2,1)} %shard_map.37) | data formatting | bytes 262144

commit v2 on v1

--- a/solution.py
+++ b/solution.py
@@ -10,13 +10,17 @@
 
 OB = 2
 LANES = 128
+CODES = 256.0
+SCALE = 256.0 * 127.0
+TINY = 1e-30
 ROWS = 8
 
 
 def ladder_kernel(
     n_row, n_col, a_dev,
     blocks, amp_hbm, int_hbm, out_ref,
-    amp, ints, lhs, prod, turned, inbox, from_left, from_right,
+    amp, ints, lhs, prod, turned, inbox,
+    main_out, rest_out, main_left, rest_left, main_right, rest_right,
     amp_sem, int_sem, x_send, x_recv, r_send, r_recv, l_send, l_recv,
 ):
     row = lax.axis_index("row")
@@ -95,7 +99,7 @@
                 prod[t, pl.ds(a, 2 * pairs, stride=a_dev), :] = got[:, t * LANES:(t + 1) * LANES]
             return carry
 
-        lax.fori_loop(0, part // width, one, 0, unroll=2)
+        lax.fori_loop(0, part // width, one, 0, unroll=8)
 
     n_near = jnp.where(col > 0, 1, 0) + jnp.where(col < n_col - 1, 1, 0)
     pl.semaphore_wait(barrier, n_row - 1 + n_near)
@@ -103,34 +107,61 @@
     def order(s):
         return jnp.where(col < n_col // 2, n_col - 1 - s, s)
 
-    def x_copy(d, p):
+    def x_copy(d, g, p):
         peer = lax.rem(row + p, n_row)
         return pltpu.make_async_remote_copy(
-            src_ref=turned.at[pl.ds(d * groups, groups), pl.ds(pl.multiple_of(peer * a_dev, a_dev), a_dev), :],
-            dst_ref=inbox.at[d, row],
-            send_sem=x_send.at[d, p],
-            recv_sem=x_recv.at[d, p],
+            src_ref=turned.at[d * groups + g, pl.ds(pl.multiple_of(peer * a_dev, a_dev), a_dev), :],
+            dst_ref=inbox.at[d, g, row],
+            send_sem=x_send.at[d, g, p],
+            recv_sem=x_recv.at[d, g, p],
             device_id={"row": peer},
         )
 
-    chunk = share * a_dev
-
-    def mine(d, t, start=0, size=chunk):
-        return prod.at[t, pl.ds(pl.multiple_of(d * chunk + start, a_dev), size)]
-
-    def right_copy(d, t):
-        return pltpu.make_async_remote_copy(
-            src_ref=mine(d, t), dst_ref=from_left.at[d, t],
-            send_sem=r_send.at[d, t], recv_sem=r_recv.at[d, t],
-            device_id={"col": col + 1},
-        )
-
-    def left_copy(d, t):
-        return pltpu.make_async_remote_copy(
-            src_ref=mine(d, t), dst_ref=from_right.at[d, t],
-            send_sem=l_send.at[d, t], recv_sem=l_recv.at[d, t],
-            device_id={"col": col - 1},
-        )
+    def z_copies(d, g, right):
+        send, recv = (r_send, r_recv) if right else (l_send, l_recv)
+        main_in, rest_in = (main_left, rest_left) if right else (main_right, rest_right)
+        to = col + 1 if right else col - 1
+        return [
+            pltpu.make_async_remote_copy(
+                src_ref=src.at[d, g], dst_ref=dst.at[d, g],
+                send_sem=send.at[d, g, i], recv_sem=recv.at[d, g, i],
+                device_id={"col": to},
+            )
+            for i, (src, dst) in enumerate(((main_out, main_in), (rest_out, rest_in)))
+        ]
+
+    def held(d, g, t):
+        start = pl.multiple_of(d * (share * a_dev) + g * LANES, LANES)
+        return prod.at[t, pl.ds(start, LANES)]
+
+    half = tiles // 2
+
+    def add_from(d, g, right):
+        for copy in z_copies(d, g, right):
+            copy.wait_recv()
+        main_in, rest_in = (main_left, rest_left) if right else (main_right, rest_right)
+        for t in range(half):
+            word = rest_in[d, g, t].astype(jnp.int32).astype(jnp.float32)
+            high = jnp.round(word * (1.0 / CODES))
+            for place, code in ((t, high), (t + half, word - high * CODES)):
+                main = main_in[d, g, place].astype(jnp.float32)
+                step = jnp.maximum(jnp.abs(main), TINY) * (1.0 / SCALE)
+                here = held(d, g, place)
+                here[...] = here[...] + (main + code * step)
+
+    def send_on(d, g, right):
+        for t in range(half):
+            codes = []
+            for place in (t, t + half):
+                value = held(d, g, place)[...]
+                main = value.astype(jnp.bfloat16)
+                main_out[d, g, place] = main
+                main = main.astype(jnp.float32)
+                codes.append(jnp.round((value - main) * (SCALE / jnp.maximum(jnp.abs(main), TINY))))
+            word = codes[0] * CODES + codes[1]
+            rest_out[d, g, t] = word.astype(jnp.int32).astype(jnp.int16)
+        for copy in z_copies(d, g, right):
+            copy.start()
 
     def turn(s, carry):
         d = order(s)
@@ -140,11 +171,11 @@
                 block = prod[t, pl.ds(pl.multiple_of(start, LANES), LANES), :]
                 turned[d * groups + g, t * LANES:(t + 1) * LANES, :] = block.T
 
-        def post(p, inner):
-            x_copy(d, p).start()
-            return inner
-
-        lax.fori_loop(1, n_row, post, 0)
+            def post(p, inner, g=g):
+                x_copy(d, g, p).start()
+                return inner
+
+            lax.fori_loop(1, n_row, post, 0)
         return carry
 
     lax.fori_loop(0, n_col, turn, 0)
@@ -154,78 +185,78 @@
     def combine(s, carry):
         d = order(s)
         for g in range(groups):
-            inbox[d, row, g] = turned[d * groups + g, pl.ds(pl.multiple_of(row * a_dev, a_dev), a_dev), :]
-        for t in range(tiles):
-            for j in range(per_tile):
-                source = t * per_tile + j
-
-                @pl.when(source != row)
-                def _(source=source):
-                    x_copy(d, lax.rem(row - source + n_row, n_row)).wait_recv()
-
-            for g in range(groups):
-                parts = [inbox[d, t * per_tile + j, g] for j in range(per_tile)]
+            inbox[d, g, row] = turned[d * groups + g, pl.ds(pl.multiple_of(row * a_dev, a_dev), a_dev), :]
+
+            def arrived(p, inner, g=g):
+                x_copy(d, g, p).wait_recv()
+                return inner
+
+            lax.fori_loop(1, n_row, arrived, 0)
+            for t in range(tiles):
+                parts = [inbox[d, g, t * per_tile + j] for j in range(per_tile)]
+                sums = []
                 for q in range(per_tile):
-                    merged = parts[q] if q == 0 else pltpu.roll(parts[0], (-q * a_dev) % LANES, 1)
+                    merged = pltpu.roll(parts[0], (-q * a_dev) % LANES, 1) if q else parts[0]
                     for j in range(1, per_tile):
                         shift = ((j - q) * a_dev) % LANES
                         moved = pltpu.roll(parts[j], shift, 1) if shift else parts[j]
                         merged = jnp.where(piece == j, moved, merged)
-                    here = mine(d, t, (g * per_tile + q) * a_dev, a_dev)
-                    here[...] = here[...] + merged
+                    sums.append(merged)
+                here = held(d, g, t)
+                here[...] = here[...] + jnp.concatenate(sums, axis=0)
 
             @pl.when(d > col)
-            def _():
+            def _(g=g):
                 @pl.when(col > 0)
                 def _():
-                    right_copy(d, t).wait_recv()
-                    mine(d, t)[...] = mine(d, t)[...] + from_left[d, t]
-
-                right_copy(d, t).start()
+                    add_from(d, g, True)
+
+                send_on(d, g, True)
 
             @pl.when(d < col)
-            def _():
+            def _(g=g):
                 @pl.when(col < n_col - 1)
                 def _():
-                    left_copy(d, t).wait_recv()
-                    mine(d, t)[...] = mine(d, t)[...] + from_right[d, t]
-
-                left_copy(d, t).start()
+                    add_from(d, g, False)
+
+                send_on(d, g, False)
 
         return carry
 
     lax.fori_loop(0, n_col, combine, 0)
 
+    for g in range(groups):
+        @pl.when(col > 0)
+        def _(g=g):
+            add_from(col, g, True)
+
+        @pl.when(col < n_col - 1)
+        def _(g=g):
+            add_from(col, g, False)
+
     for t in range(tiles):
-        @pl.when(col > 0)
-        def _(t=t):
-            right_copy(col, t).wait_recv()
-            mine(col, t)[...] = mine(col, t)[...] + from_left[col, t]
-
-        @pl.when(col < n_col - 1)
-        def _(t=t):
-            left_copy(col, t).wait_recv()
-            mine(col, t)[...] = mine(col, t)[...] + from_right[col, t]
-
         for a in range(a_dev):
-            value = prod[t, pl.ds(col * chunk + a, share, stride=a_dev), :]
+            value = prod[t, pl.ds(col * (share * a_dev) + a, share, stride=a_dev), :]
             at = a * width + t * LANES
             out_ref[:, at:at + LANES] = value.astype(out_ref.dtype)
 
     def finish(d, carry):
-        def sent(p, inner):
-            x_copy(d, p).wait_send()
-            return inner
-
-        lax.fori_loop(1, n_row, sent, 0)
-        for t in range(tiles):
+        for g in range(groups):
+            def sent(p, inner, g=g):
+                x_copy(d, g, p).wait_send()
+                return inner
+
+            lax.fori_loop(1, n_row, sent, 0)
+
             @pl.when(d > col)
-            def _(t=t):
-                right_copy(d, t).wait_send()
+            def _(g=g):
+                for copy in z_copies(d, g, True):
+                    copy.wait_send()
 
             @pl.when(d < col)
-            def _(t=t):
-                left_copy(d, t).wait_send()
+            def _(g=g):
+                for copy in z_copies(d, g, False):
+                    copy.wait_send()
 
         return carry
 
@@ -245,6 +276,10 @@
     n_parts = 4
     f32 = jnp.float32
     dma = pltpu.SemaphoreType.DMA
+    coded = [
+        pltpu.VMEM((n_col, groups, tiles, LANES, LANES), jnp.bfloat16),
+        pltpu.VMEM((n_col, groups, tiles // 2, LANES, LANES), jnp.int16),
+    ]
     return pl.pallas_call(
         functools.partial(ladder_kernel, n_row, n_col, a_dev),
         out_shape=jax.ShapeDtypeStruct((share, local), jnp.bfloat16),
@@ -260,17 +295,16 @@
             pltpu.VMEM((2 * pairs, depth), f32),
             pltpu.VMEM((tiles, 2 * pairs * a_dev, LANES), f32),
             pltpu.VMEM((n_col * groups, width, LANES), f32),
-            pltpu.VMEM((n_col, n_row, groups, a_dev, LANES), f32),
-            pltpu.VMEM((n_col, tiles, share * a_dev, LANES), f32),
-            pltpu.VMEM((n_col, tiles, share * a_dev, LANES), f32),
+            pltpu.VMEM((n_col, groups, n_row, a_dev, LANES), f32),
+            *coded, *coded, *coded,
             dma(()),
             dma((n_parts,)),
-            dma((n_col, n_row)),
-            dma((n_col, n_row)),
-            dma((n_col, tiles)),
-            dma((n_col, tiles)),
-            dma((n_col, tiles)),
-            dma((n_col, tiles)),
+            dma((n_col, groups, n_row)),
+            dma((n_col, groups, n_row)),
+            dma((n_col, groups, 2)),
+            dma((n_col, groups, 2)),
+            dma((n_col, groups, 2)),
+            dma((n_col, groups, 2)),
         ],
         compiler_params=pltpu.CompilerParams(
             collective_id=0, has_side_effects=True, vmem_limit_bytes=67043328

time: 41.4 us -> 35.9 us (0.87)
  Pallas kernels: 39.7 us -> 34.2 us
    pallas_call x1, Pallas kernels: 39.7 us -> 34.2 us  [on_device(): pl.pallas_call(functools.partial(ladder_kernel, n_row, n_col, a_dev), out...]
where the time goes in v2:
time: 35.9 us; the launch traced here: 35.7 us
  Pallas kernels  34.2 us (95%)
  local copies, waits for them, and re-layouts  1.57 us (4%)
    pallas_call x1, Pallas kernels, on_device(): pl.pallas_call(functools.partial(ladder_kernel, n_row, n_col, a_dev), out...  34.2 us
    unnamed x1, local copies, waits for them, and re-layouts  1.57 us

profile of v2, /device:TPU:0, one launch (start us, length us, event | category | flops | bytes accessed | tf_op | source)
XLA Modules:
  0.0 35.7 jit_solution(14230834451903403718)
XLA Ops:
  0.0 34.2 %shard_map.37 = bf16[8,8192]{1,0:T(8,128)(2,1)} custom-call(s32[2,8]{1,0:T(2,128)} %bitcast.3, bf16[100,192,100]{2,1,0:T(8,128)(2,1)} %bitcast.2, bf16[192,8192]{1,0:T(8,128)(2,1)} %int_hbm.1), custom_call_target="tpu_custom_call" | custom-call | tf_op jit(solution)/shard_map/pallas_call | solution.py:283
  34.2 1.6 %copy.5 = bf16[8,8192]{1,0:T(8,128)(2,1)} copy(bf16[8,8192]{1,0:T(8,128)(2,1)} %shard_map.37) | data formatting | bytes 262144

commit v3 on v2

--- a/solution.py
+++ b/solution.py
@@ -88,24 +88,41 @@
         lhs[pairs + tile * ROWS:pairs + (tile + 1) * ROWS, :] = swapped
     rows = lhs[...].astype(jnp.bfloat16)
 
+    def multiply(i, first):
+        block = rows[first:first + pairs]
+
+        def one(step, carry):
+            a = i * (part // width) + step
+            panel = ints[:, pl.ds(pl.multiple_of(a * width, width), width)]
+            got = jnp.dot(block, panel, preferred_element_type=jnp.float32)
+            for t in range(tiles):
+                prod[t, pl.ds(first * a_dev + a, pairs, stride=a_dev), :] = got[:, t * LANES:(t + 1) * LANES]
+            return carry
+
+        lax.fori_loop(0, part // width, one, 0, unroll=8)
+
     for i in range(n_parts):
         int_copies[i].wait()
-
-        def one(step, carry, i=i):
-            a = i * (part // width) + step
-            panel = ints[:, pl.ds(pl.multiple_of(a * width, width), width)]
-            got = jnp.dot(rows, panel, preferred_element_type=jnp.float32)
-            for t in range(tiles):
-                prod[t, pl.ds(a, 2 * pairs, stride=a_dev), :] = got[:, t * LANES:(t + 1) * LANES]
-            return carry
-
-        lax.fori_loop(0, part // width, one, 0, unroll=8)
+        multiply(i, pairs)
 
     n_near = jnp.where(col > 0, 1, 0) + jnp.where(col < n_col - 1, 1, 0)
     pl.semaphore_wait(barrier, n_row - 1 + n_near)
 
-    def order(s):
-        return jnp.where(col < n_col // 2, n_col - 1 - s, s)
+    to_right = n_col - 1 - col
+    near = jnp.minimum(col, to_right)
+    lone = (jnp.maximum(col, to_right) - near) * groups
+    outward = jnp.where(to_right >= col, 1, -1)
+
+    def unit(k):
+        rest = jnp.maximum(k - lone, 0)
+        distance = near - rest // (2 * groups)
+        within = rest % (2 * groups)
+        side = jnp.where(within % 2 == 0, -outward, outward)
+        is_lone = k < lone
+        is_own = distance == 0
+        shift = jnp.where(is_lone, outward * (near + (lone - 1 - k) // groups + 1), side * distance)
+        g = jnp.where(is_lone, k % groups, jnp.where(is_own, within, within // 2))
+        return col + shift, g
 
     def x_copy(d, g, p):
         peer = lax.rem(row + p, n_row)
@@ -163,67 +180,68 @@
         for copy in z_copies(d, g, right):
             copy.start()
 
-    def turn(s, carry):
-        d = order(s)
-        for g in range(groups):
-            start = (pairs + d * share + g * per_tile) * a_dev
-            for t in range(tiles):
-                block = prod[t, pl.ds(pl.multiple_of(start, LANES), LANES), :]
-                turned[d * groups + g, t * LANES:(t + 1) * LANES, :] = block.T
-
-            def post(p, inner, g=g):
-                x_copy(d, g, p).start()
-                return inner
-
-            lax.fori_loop(1, n_row, post, 0)
+    def turn(k, carry):
+        d, g = unit(k)
+        start = (pairs + d * share + g * per_tile) * a_dev
+        for t in range(tiles):
+            block = prod[t, pl.ds(pl.multiple_of(start, LANES), LANES), :]
+            turned[d * groups + g, t * LANES:(t + 1) * LANES, :] = block.T
+
+        def post(p, inner):
+            x_copy(d, g, p).start()
+            return inner
+
+        lax.fori_loop(1, n_row, post, 0)
         return carry
 
-    lax.fori_loop(0, n_col, turn, 0)
+    lax.fori_loop(0, n_col * groups, turn, 0)
+
+    for i in range(n_parts):
+        multiply(i, 0)
 
     piece = lax.broadcasted_iota(jnp.int32, (a_dev, LANES), 1) // a_dev
 
-    def combine(s, carry):
-        d = order(s)
-        for g in range(groups):
-            inbox[d, g, row] = turned[d * groups + g, pl.ds(pl.multiple_of(row * a_dev, a_dev), a_dev), :]
-
-            def arrived(p, inner, g=g):
-                x_copy(d, g, p).wait_recv()
-                return inner
-
-            lax.fori_loop(1, n_row, arrived, 0)
-            for t in range(tiles):
-                parts = [inbox[d, g, t * per_tile + j] for j in range(per_tile)]
-                sums = []
-                for q in range(per_tile):
-                    merged = pltpu.roll(parts[0], (-q * a_dev) % LANES, 1) if q else parts[0]
-                    for j in range(1, per_tile):
-                        shift = ((j - q) * a_dev) % LANES
-                        moved = pltpu.roll(parts[j], shift, 1) if shift else parts[j]
-                        merged = jnp.where(piece == j, moved, merged)
-                    sums.append(merged)
-                here = held(d, g, t)
-                here[...] = here[...] + jnp.concatenate(sums, axis=0)
-
-            @pl.when(d > col)
-            def _(g=g):
-                @pl.when(col > 0)
-                def _():
-                    add_from(d, g, True)
-
-                send_on(d, g, True)
-
-            @pl.when(d < col)
-            def _(g=g):
-                @pl.when(col < n_col - 1)
-                def _():
-                    add_from(d, g, False)
-
-                send_on(d, g, False)
+    def combine(k, carry):
+        d, g = unit(k)
+        inbox[d, g, row] = turned[d * groups + g, pl.ds(pl.multiple_of(row * a_dev, a_dev), a_dev), :]
+
+        def arrived(p, inner):
+            x_copy(d, g, p).wait_recv()
+            return inner
+
+        lax.fori_loop(1, n_row, arrived, 0)
+        for t in range(tiles):
+            parts = [inbox[d, g, t * per_tile + j] for j in range(per_tile)]
+            sums = []
+            for q in range(per_tile):
+                merged = pltpu.roll(parts[0], (-q * a_dev) % LANES, 1) if q else parts[0]
+                for j in range(1, per_tile):
+                    shift = ((j - q) * a_dev) % LANES
+                    moved = pltpu.roll(parts[j], shift, 1) if shift else parts[j]
+                    merged = jnp.where(piece == j, moved, merged)
+                sums.append(merged)
+            here = held(d, g, t)
+            here[...] = here[...] + jnp.concatenate(sums, axis=0)
+
+        @pl.when(d > col)
+        def _():
+            @pl.when(col > 0)
+            def _():
+                add_from(d, g, True)
+
+            send_on(d, g, True)
+
+        @pl.when(d < col)
+        def _():
+            @pl.when(col < n_col - 1)
+            def _():
+                add_from(d, g, False)
+
+            send_on(d, g, False)
 
         return carry
 
-    lax.fori_loop(0, n_col, combine, 0)
+    lax.fori_loop(0, n_col * groups, combine, 0)
 
     for g in range(groups):
         @pl.when(col > 0)

time: 35.9 us -> 33.4 us (0.930)
  Pallas kernels: 34.2 us -> 31.7 us
    pallas_call x1, Pallas kernels: 34.2 us -> 31.7 us  [on_device(): pl.pallas_call(functools.partial(ladder_kernel, n_row, n_col, a_dev), out...]
where the time goes in v3:
time: 33.4 us; the launch traced here: 33.3 us
  Pallas kernels  31.7 us (95%)
  local copies, waits for them, and re-layouts  1.57 us (5%)
    pallas_call x1, Pallas kernels, on_device(): pl.pallas_call(functools.partial(ladder_kernel, n_row, n_col, a_dev), out...  31.7 us
    unnamed x1, local copies, waits for them, and re-layouts  1.57 us

profile of v3, /device:TPU:0, one launch (start us, length us, event | category | flops | bytes accessed | tf_op | source)
XLA Modules:
  0.0 33.3 jit_solution(15582780502579798814)
XLA Ops:
  0.0 31.7 %shard_map.37 = bf16[8,8192]{1,0:T(8,128)(2,1)} custom-call(s32[2,8]{1,0:T(2,128)} %bitcast.3, bf16[100,192,100]{2,1,0:T(8,128)(2,1)} %bitcast.2, bf16[192,8192]{1,0:T(8,128)(2,1)} %int_hbm.1), custom_call_target="tpu_custom_call" | custom-call | tf_op jit(solution)/shard_map/pallas_call | solution.py:301
  31.7 1.6 %copy.5 = bf16[8,8192]{1,0:T(8,128)(2,1)} copy(bf16[8,8192]{1,0:T(8,128)(2,1)} %shard_map.37) | data formatting | bytes 262144

commit v4 on v3

--- a/solution.py
+++ b/solution.py
@@ -57,10 +57,13 @@
     for i in range(n_parts):
         cut = pl.ds(i * part, part)
         copy = pltpu.make_async_copy(int_hbm.at[:, cut], ints.at[:, cut], int_sem.at[i])
+        if i < n_parts // 2:
+            copy.start()
+        int_copies.append(copy)
+
+    amp_copy.wait()
+    for copy in int_copies[n_parts // 2:]:
         copy.start()
-        int_copies.append(copy)
-
-    amp_copy.wait()
     spot_row = lax.broadcasted_iota(jnp.int32, (ROWS, occ), 0)
     spot_col = lax.broadcasted_iota(jnp.int32, (ROWS, occ), 1)
 
@@ -74,22 +77,26 @@
         )
 
     per_rows = ROWS // (OB * OB)
-    for tile in range(pairs // ROWS):
-        direct = jnp.zeros((ROWS, lhs.shape[1]), jnp.float32)
-        swapped = direct
-        for k in range(per_rows):
-            upper = blocks[0, tile * per_rows + k] * OB
-            lower = blocks[1, tile * per_rows + k] * OB
-            base = k * OB * OB
-            for m in range(OB):
-                direct += take([(base + m * OB + v, lower + v) for v in range(OB)], upper + m)
-                swapped += take([(base + u * OB + m, upper + u) for u in range(OB)], lower + m)
-        lhs[tile * ROWS:(tile + 1) * ROWS, :] = direct
-        lhs[pairs + tile * ROWS:pairs + (tile + 1) * ROWS, :] = swapped
-    rows = lhs[...].astype(jnp.bfloat16)
+
+    def gather(mirrored):
+        for tile in range(pairs // ROWS):
+            found = jnp.zeros((ROWS, lhs.shape[1]), jnp.float32)
+            for k in range(per_rows):
+                upper = blocks[0, tile * per_rows + k] * OB
+                lower = blocks[1, tile * per_rows + k] * OB
+                base = k * OB * OB
+                for m in range(OB):
+                    if mirrored:
+                        found += take([(base + u * OB + m, upper + u) for u in range(OB)], lower + m)
+                    else:
+                        found += take([(base + m * OB + v, lower + v) for v in range(OB)], upper + m)
+            at = (pairs if mirrored else 0) + tile * ROWS
+            lhs[at:at + ROWS, :] = found
+
+    gather(True)
 
     def multiply(i, first):
-        block = rows[first:first + pairs]
+        block = lhs[first:first + pairs, :].astype(jnp.bfloat16)
 
         def one(step, carry):
             a = i * (part // width) + step
@@ -196,6 +203,7 @@
 
     lax.fori_loop(0, n_col * groups, turn, 0)
 
+    gather(False)
     for i in range(n_parts):
         multiply(i, 0)
 

time: 33.4 us -> 32.6 us (0.976)
  Pallas kernels: 31.7 us -> 30.8 us
    pallas_call x1, Pallas kernels: 31.7 us -> 30.8 us  [on_device(): pl.pallas_call(functools.partial(ladder_kernel, n_row, n_col, a_dev), out...]
where the time goes in v4:
time: 32.6 us; the launch traced here: 32.4 us
  Pallas kernels  30.8 us (94%)
  local copies, waits for them, and re-layouts  1.57 us (5%)
    pallas_call x1, Pallas kernels, on_device(): pl.pallas_call(functools.partial(ladder_kernel, n_row, n_col, a_dev), out...  30.8 us
    unnamed x1, local copies, waits for them, and re-layouts  1.57 us

profile of v4, /device:TPU:0, one launch (start us, length us, event | category | flops | bytes accessed | tf_op | source)
XLA Modules:
  0.0 32.4 jit_solution(8098971703113956790)
XLA Ops:
  0.0 30.8 %shard_map.37 = bf16[8,8192]{1,0:T(8,128)(2,1)} custom-call(s32[2,8]{1,0:T(2,128)} %bitcast.3, bf16[100,192,100]{2,1,0:T(8,128)(2,1)} %bitcast.2, bf16[192,8192]{1,0:T(8,128)(2,1)} %int_hbm.1), custom_call_target="tpu_custom_call" | custom-call | tf_op jit(solution)/shard_map/pallas_call | solution.py:309
  30.8 1.6 %copy.5 = bf16[8,8192]{1,0:T(8,128)(2,1)} copy(bf16[8,8192]{1,0:T(8,128)(2,1)} %shard_map.37) | data formatting | bytes 262144

commit v5 on v4

--- a/solution.py
+++ b/solution.py
@@ -131,8 +131,20 @@
         g = jnp.where(is_lone, k % groups, jnp.where(is_own, within, within // 2))
         return col + shift, g
 
+    def partner(p):
+        if n_row & (n_row - 1):
+            return lax.rem(row + p, n_row)
+        peer, bit = row, 1
+        while bit < n_row:
+            if p & bit:
+                peer = peer + bit - 2 * bit * ((row // bit) % 2)
+            bit *= 2
+        return peer
+
+    steps = sorted(range(1, n_row), key=lambda p: (-bin(p // 2).count('1'), p))
+
     def x_copy(d, g, p):
-        peer = lax.rem(row + p, n_row)
+        peer = partner(p)
         return pltpu.make_async_remote_copy(
             src_ref=turned.at[d * groups + g, pl.ds(pl.multiple_of(peer * a_dev, a_dev), a_dev), :],
             dst_ref=inbox.at[d, g, row],
@@ -194,11 +206,8 @@
             block = prod[t, pl.ds(pl.multiple_of(start, LANES), LANES), :]
             turned[d * groups + g, t * LANES:(t + 1) * LANES, :] = block.T
 
-        def post(p, inner):
+        for p in steps:
             x_copy(d, g, p).start()
-            return inner
-
-        lax.fori_loop(1, n_row, post, 0)
         return carry
 
     lax.fori_loop(0, n_col * groups, turn, 0)
@@ -213,11 +222,8 @@
         d, g = unit(k)
         inbox[d, g, row] = turned[d * groups + g, pl.ds(pl.multiple_of(row * a_dev, a_dev), a_dev), :]
 
-        def arrived(p, inner):
+        for p in steps:
             x_copy(d, g, p).wait_recv()
-            return inner
-
-        lax.fori_loop(1, n_row, arrived, 0)
         for t in range(tiles):
             parts = [inbox[d, g, t * per_tile + j] for j in range(per_tile)]
             sums = []
@@ -268,11 +274,8 @@
 
     def finish(d, carry):
         for g in range(groups):
-            def sent(p, inner, g=g):
+            for p in steps:
                 x_copy(d, g, p).wait_send()
-                return inner
-
-            lax.fori_loop(1, n_row, sent, 0)
 
             @pl.when(d > col)
             def _(g=g):

time: 32.6 us -> 32.1 us (0.985)
  Pallas kernels: 30.8 us -> 30.4 us
    pallas_call x1, Pallas kernels: 30.8 us -> 30.4 us  [on_device(): pl.pallas_call(functools.partial(ladder_kernel, n_row, n_col, a_dev), out...]
where the time goes in v5:
time: 32.1 us; the launch traced here: 32 us
  Pallas kernels  30.4 us (95%)
  local copies, waits for them, and re-layouts  1.57 us (5%)
    pallas_call x1, Pallas kernels, on_device(): pl.pallas_call(functools.partial(ladder_kernel, n_row, n_col, a_dev), out...  30.4 us
    unnamed x1, local copies, waits for them, and re-layouts  1.57 us

profile of v5, /device:TPU:0, one launch (start us, length us, event | category | flops | bytes accessed | tf_op | source)
XLA Modules:
  0.0 32.0 jit_solution(12852793791791357631)
XLA Ops:
  0.0 30.4 %shard_map.37 = bf16[8,8192]{1,0:T(8,128)(2,1)} custom-call(s32[2,8]{1,0:T(2,128)} %bitcast.3, bf16[100,192,100]{2,1,0:T(8,128)(2,1)} %bitcast.2, bf16[192,8192]{1,0:T(8,128)(2,1)} %int_hbm.1), custom_call_target="tpu_custom_call" | custom-call | tf_op jit(solution)/shard_map/pallas_call | solution.py:312
  30.4 1.6 %copy.5 = bf16[8,8192]{1,0:T(8,128)(2,1)} copy(bf16[8,8192]{1,0:T(8,128)(2,1)} %shard_map.37) | data formatting | bytes 262144
